TPU v7x, 128 devices: a whole 4x4x4 slice. The times are simulated.
128 devices in a mesh: req: 32 (over y, z, core), tp: 4 (over x).
Axes of the slice: x: 4, y: 4, z: 4, core: 2. Of those that a mesh axis runs over, the one named last changes fastest.
Arguments:
- tokens: bfloat16 [512, 2048], P('req'), may hold values from -6 to 6
- lengths: int32 [512], P('req'), may hold values from 1 to 8192, 131072 in all
- pool_order: int32 [512], replicated, may hold values from 0 to 511, each once
- positions: int32 [512], P('req'), may hold values from 0 to 16383
- slot_mask: int32 [131072], P('req'), may hold values 0 or 1
- kv_cache: bfloat16 [131072, 2, 1024], P('req', None, 'tp'), may hold values from -420 to 420
- attn_gain: bfloat16 [2048], replicated, may hold values from 0.25 to 1.75
- w_query: bfloat16 [2048, 2048], P(None, 'tp'), may hold values from -0.125 to 0.125
- w_key: bfloat16 [2048, 1024], P(None, 'tp'), may hold values from -0.125 to 0.125
- w_value: bfloat16 [2048, 1024], P(None, 'tp'), may hold values from -0.125 to 0.125
- w_out: bfloat16 [2048, 2048], P('tp'), may hold values from -0.125 to 0.125
- ffn_gain: bfloat16 [2048], replicated, may hold values from 0.25 to 1.75
- w_gate: bfloat16 [2048, 4096], P(None, 'tp'), may hold values from -0.125 to 0.125
- w_up: bfloat16 [2048, 4096], P(None, 'tp'), may hold values from -0.125 to 0.125
- w_down: bfloat16 [4096, 2048], P('tp'), may hold values from -0.09375 to 0.09375
Outputs:
- hidden_out: float32 [512, 2048], P('req')
- new_kv: float32 [512, 2, 1024], P('req', None, 'tp')
Inputs may be any that keep to these rules, and one draw needn't show every extreme that they name: The lengths add up to 131072, so the requests' caches fill the pool end to end; the largest is exactly 8192. `pool_order`: each request appears exactly once.
All inputs are finite; a program needn't handle non-finite values. No bound on the sum of `lengths` or of `slot_mask` on one device may be relied on, other than what follows from the above.
Results may differ from a plain program's by a relative error of at most 0.013.
The roundings to bfloat16 on the way count: a program that leaves them out, or rounds other values in their place, can miss the bound.
Values may be sent and summed in bfloat16 or wider, within the bound.
A program may use at most 192 MiB of HBM per device.

v0:
```python
import math
import jax
import jax.numpy as jnp
from jax import lax
from jax.sharding import PartitionSpec as P

HEAD_DIM = 128
ROPE_BASE = 1000000.0
EPS = 1e-05
FLOOR = -1e30


def joined(part, axis, combine):
    gathered = jax.tree.map(lambda a: lax.all_gather(a, axis), part)

    def take(source):
        return jax.tree.map(lambda a: lax.dynamic_index_in_dim(a, source, 0, False), gathered)

    return lax.fori_loop(
        1, lax.axis_size(axis), lambda source, state: combine(state, take(source)), take(0)
    )


def rms_norm(rows, gain):
    mean_sq = jnp.mean(rows * rows, axis=-1, keepdims=True)
    return rows * lax.rsqrt(mean_sq + EPS) * gain.astype(jnp.float32)


def rotate(vectors, places):
    width = vectors.shape[-1]
    half = width // 2
    freq = ROPE_BASE ** (-(jnp.arange(half, dtype=jnp.float32) * 2.0) / width)
    angle = places.astype(jnp.float32)[:, None] * freq[None, :]
    cosine = jnp.cos(angle)[:, None, :]
    sine = jnp.sin(angle)[:, None, :]
    first = vectors[..., :half]
    second = vectors[..., half:]
    return jnp.concatenate(
        [first * cosine - second * sine, second * cosine + first * sine], axis=-1
    )


def combine_parts(first, second):
    peak = jnp.maximum(first[0], second[0])
    left = jnp.exp(first[0] - peak)
    right = jnp.exp(second[0] - peak)
    return (
        peak,
        first[1] * left + second[1] * right,
        first[2] * left[..., None] + second[2] * right[..., None],
    )


def per_device(
    tokens,
    lengths,
    pool_order,
    positions,
    slot_mask,
    kv_cache,
    attn_gain,
    w_query,
    w_key,
    w_value,
    w_out,
    ffn_gain,
    w_gate,
    w_up,
    w_down,
):
    count = tokens.shape[0]
    head_dim = HEAD_DIM
    kv_local = w_key.shape[1] // head_dim
    q_local = w_query.shape[1] // head_dim
    group = q_local // kv_local
    slot_count = kv_cache.shape[0]
    scale = 1.0 / math.sqrt(head_dim)
    highest = lax.Precision.HIGHEST
    all_lengths = lax.all_gather(lengths, "req", axis=0, tiled=True)
    total_reqs = all_lengths.shape[0]
    ordered = all_lengths[pool_order]
    ends = jnp.cumsum(ordered)
    base = lax.axis_index("req") * slot_count
    slot_ids = base + jnp.arange(slot_count, dtype=jnp.int32)
    place = jnp.searchsorted(ends, slot_ids, side="right")
    owner = pool_order[place]
    belongs = owner[:, None] == jnp.arange(total_reqs, dtype=jnp.int32)[None, :]
    belongs_f = belongs.astype(jnp.float32)
    rows = tokens.astype(jnp.float32)
    normed = rms_norm(rows, attn_gain).astype(jnp.bfloat16)
    query = rotate(
        jnp.dot(normed, w_query, preferred_element_type=jnp.float32).reshape(
            count, q_local, head_dim
        ),
        positions,
    ).astype(jnp.bfloat16)
    key_full = rotate(
        jnp.dot(normed, w_key, preferred_element_type=jnp.float32).reshape(
            count, kv_local, head_dim
        ),
        positions,
    )
    value_full = jnp.dot(normed, w_value, preferred_element_type=jnp.float32)
    new_kv = jnp.stack([key_full.reshape(count, kv_local * head_dim), value_full], axis=1)
    new_key = key_full.astype(jnp.bfloat16)
    new_value = value_full.astype(jnp.bfloat16)
    everyone = lax.all_gather(query.reshape(count, q_local * head_dim), "req", axis=0, tiled=True)
    picked = everyone[owner].reshape(slot_count, kv_local, group, head_dim)
    keys = kv_cache[:, 0, :].reshape(slot_count, kv_local, head_dim)
    values = kv_cache[:, 1, :].reshape(slot_count, kv_local, head_dim)
    scores = jnp.einsum("skgd,skd->skg", picked, keys, preferred_element_type=jnp.float32) * scale
    live = (slot_mask == 1)[:, None, None]
    scores = jnp.where(live, scores, FLOOR)
    peak_heads = []
    for head in range(kv_local):
        masked = jnp.where(belongs[:, :, None], scores[:, head, :][:, None, :], FLOOR)
        peak_heads.append(jnp.max(masked, axis=0))
    peak = jnp.stack(peak_heads, axis=1)
    weights = jnp.where(live, jnp.exp(scores - peak[owner]), 0.0)
    total = jnp.dot(
        belongs_f.T,
        weights.reshape(slot_count, kv_local * group),
        precision=highest,
        preferred_element_type=jnp.float32,
    ).reshape(total_reqs, kv_local, group)
    sum_heads = []
    for head in range(kv_local):
        spread = belongs_f[:, :, None] * weights[:, head, :][:, None, :]
        head_values = values[:, head, :].astype(jnp.float32)
        sum_heads.append(
            jnp.einsum(
                "srg,sd->rgd",
                spread,
                head_values,
                precision=highest,
                preferred_element_type=jnp.float32,
            )
        )
    summed = jnp.stack(sum_heads, axis=1)
    start = lax.axis_index("req") * count
    merged = joined((peak, total, summed), "req", combine_parts)
    own_peak = lax.dynamic_slice_in_dim(merged[0], start, count, 0)
    own_total = lax.dynamic_slice_in_dim(merged[1], start, count, 0)
    own_sum = lax.dynamic_slice_in_dim(merged[2], start, count, 0)
    own_query = query.reshape(count, kv_local, group, head_dim)
    own_score = (
        jnp.einsum("nkgd,nkd->nkg", own_query, new_key, preferred_element_type=jnp.float32) * scale
    )
    final_peak = jnp.maximum(own_peak, own_score)
    old_part = jnp.exp(own_peak - final_peak)
    new_part = jnp.exp(own_score - final_peak)
    denom = own_total * old_part + new_part
    numer = own_sum * old_part[..., None] + new_part[..., None] * new_value.reshape(
        count, kv_local, 1, head_dim
    ).astype(jnp.float32)
    context = (numer / denom[..., None]).reshape(count, q_local * head_dim).astype(jnp.bfloat16)
    partial_attn = jnp.dot(context, w_out, preferred_element_type=jnp.float32)
    mid = rows + lax.psum(partial_attn, "tp")
    normed_mid = rms_norm(mid, ffn_gain).astype(jnp.bfloat16)
    gate = jnp.dot(normed_mid, w_gate, preferred_element_type=jnp.float32)
    upper = jnp.dot(normed_mid, w_up, preferred_element_type=jnp.float32)
    act = (jax.nn.silu(gate) * upper).astype(jnp.bfloat16)
    down_part = jnp.dot(act, w_down, preferred_element_type=jnp.float32)
    hidden_out = mid + lax.psum(down_part, "tp")
    return (hidden_out, new_kv)


def solution(mesh):
    placed = (
        P("req", None),
        P("req"),
        P(),
        P("req"),
        P("req"),
        P("req", None, "tp"),
        P(),
        P(None, "tp"),
        P(None, "tp"),
        P(None, "tp"),
        P("tp", None),
        P(),
        P(None, "tp"),
        P(None, "tp"),
        P("tp", None),
    )
    return jax.shard_map(
        per_device,
        mesh=mesh,
        in_specs=placed,
        out_specs=(P("req", None), P("req", None, "tp")),
        check_vma=False,
    )
```

profile of v0, /device:TPU:0, one launch (start us, length us, event | category | flops | bytes accessed | tf_op | source)
XLA Modules:
  0.0 1126.8 jit_solution(8354011638535789150)
XLA Ops:
  12.5 18.3 %all-reduce = s32[512]{0:T(512)S(1)} all-reduce(s32[512]{0:T(512)S(1)} %dynamic-update-slice), channel_id=1, replica_groups=mesh['req'=32,'tp'=4] {'req'}, use_global_device_ids=true, to_apply=%add | all-reduce | flops 512 | bytes 4096
  36.3 259.8 %while.44 = (s32[]{:T(128)}, u32[4096]{0:T(1024)S(1)}, u32[4096]{0:T(1024)S(1)}, s32[512]{0:T(512)S(1)}, s32[]{:T(128)}, /*index=5*/s32[]{:T(128)}, s32[]{:T(128)}, s32[]{}) while((s32[]{:T(128)}, u32[4096]{0:T(1024)S(1)}, u32[4096]{0:T(1024)S(1)}, s32[512]{0:T(512)S(1)}, s32[]{:T(128)}, /*index=5*/s32[]{:T(128)}, s32[]{:T(128)}, ...), condition=%wide.region_3.4_spmd.clone, body=%wide.region_2.3_spmd.clone.sunk | while | flops 81924 | bytes 254065 | solution.py:85
  36.3 25.9 %gather_fusion = s32[4096]{0:T(1024)S(1)} fusion(s32[512]{0:T(512)S(1)} %get-tuple-element.479, u32[4096]{0:T(1024)S(1)} %broadcast_clamp_fusion.3), kind=kCustom, calls=%fused_computation.clone.clone.1 | custom fusion | bytes 49152 | tf_op jit(solution)/shard_map/jit(searchsorted)/jit(_searchsorted_scan_impl)/vmap(jit(_searchsorted_scan_impl))/while/body/eval_jaxpr/gather | solution.py:85
  62.3 25.9 %gather_fusion = s32[4096]{0:T(1024)S(1)} fusion(s32[512]{0:T(512)S(1)} %get-tuple-element.479, u32[4096]{0:T(1024)S(1)} %broadcast_clamp_fusion.3), kind=kCustom, calls=%fused_computation.clone.clone.1 | custom fusion | bytes 49152 | tf_op jit(solution)/shard_map/jit(searchsorted)/jit(_searchsorted_scan_impl)/vmap(jit(_searchsorted_scan_impl))/while/body/eval_jaxpr/gather | solution.py:85
  88.2 25.9 %gather_fusion = s32[4096]{0:T(1024)S(1)} fusion(s32[512]{0:T(512)S(1)} %get-tuple-element.479, u32[4096]{0:T(1024)S(1)} %broadcast_clamp_fusion.3), kind=kCustom, calls=%fused_computation.clone.clone.1 | custom fusion | bytes 49152 | tf_op jit(solution)/shard_map/jit(searchsorted)/jit(_searchsorted_scan_impl)/vmap(jit(_searchsorted_scan_impl))/while/body/eval_jaxpr/gather | solution.py:85
  114.2 25.9 %gather_fusion = s32[4096]{0:T(1024)S(1)} fusion(s32[512]{0:T(512)S(1)} %get-tuple-element.479, u32[4096]{0:T(1024)S(1)} %broadcast_clamp_fusion.3), kind=kCustom, calls=%fused_computation.clone.clone.1 | custom fusion | bytes 49152 | tf_op jit(solution)/shard_map/jit(searchsorted)/jit(_searchsorted_scan_impl)/vmap(jit(_searchsorted_scan_impl))/while/body/eval_jaxpr/gather | solution.py:85
  140.2 25.9 %gather_fusion = s32[4096]{0:T(1024)S(1)} fusion(s32[512]{0:T(512)S(1)} %get-tuple-element.479, u32[4096]{0:T(1024)S(1)} %broadcast_clamp_fusion.3), kind=kCustom, calls=%fused_computation.clone.clone.1 | custom fusion | bytes 49152 | tf_op jit(solution)/shard_map/jit(searchsorted)/jit(_searchsorted_scan_impl)/vmap(jit(_searchsorted_scan_impl))/while/body/eval_jaxpr/gather | solution.py:85
  166.2 25.9 %gather_fusion = s32[4096]{0:T(1024)S(1)} fusion(s32[512]{0:T(512)S(1)} %get-tuple-element.479, u32[4096]{0:T(1024)S(1)} %broadcast_clamp_fusion.3), kind=kCustom, calls=%fused_computation.clone.clone.1 | custom fusion | bytes 49152 | tf_op jit(solution)/shard_map/jit(searchsorted)/jit(_searchsorted_scan_impl)/vmap(jit(_searchsorted_scan_impl))/while/body/eval_jaxpr/gather | solution.py:85
  192.2 25.9 %gather_fusion = s32[4096]{0:T(1024)S(1)} fusion(s32[512]{0:T(512)S(1)} %get-tuple-element.479, u32[4096]{0:T(1024)S(1)} %broadcast_clamp_fusion.3), kind=kCustom, calls=%fused_computation.clone.clone.1 | custom fusion | bytes 49152 | tf_op jit(solution)/shard_map/jit(searchsorted)/jit(_searchsorted_scan_impl)/vmap(jit(_searchsorted_scan_impl))/while/body/eval_jaxpr/gather | solution.py:85
  218.1 25.9 %gather_fusion = s32[4096]{0:T(1024)S(1)} fusion(s32[512]{0:T(512)S(1)} %get-tuple-element.479, u32[4096]{0:T(1024)S(1)} %broadcast_clamp_fusion.3), kind=kCustom, calls=%fused_computation.clone.clone.1 | custom fusion | bytes 49152 | tf_op jit(solution)/shard_map/jit(searchsorted)/jit(_searchsorted_scan_impl)/vmap(jit(_searchsorted_scan_impl))/while/body/eval_jaxpr/gather | solution.py:85
  244.1 25.9 %gather_fusion = s32[4096]{0:T(1024)S(1)} fusion(s32[512]{0:T(512)S(1)} %get-tuple-element.479, u32[4096]{0:T(1024)S(1)} %broadcast_clamp_fusion.3), kind=kCustom, calls=%fused_computation.clone.clone.1 | custom fusion | bytes 49152 | tf_op jit(solution)/shard_map/jit(searchsorted)/jit(_searchsorted_scan_impl)/vmap(jit(_searchsorted_scan_impl))/while/body/eval_jaxpr/gather | solution.py:85
  270.1 25.9 %gather_fusion = s32[4096]{0:T(1024)S(1)} fusion(s32[512]{0:T(512)S(1)} %get-tuple-element.479, u32[4096]{0:T(1024)S(1)} %broadcast_clamp_fusion.3), kind=kCustom, calls=%fused_computation.clone.clone.1 | custom fusion | bytes 49152 | tf_op jit(solution)/shard_map/jit(searchsorted)/jit(_searchsorted_scan_impl)/vmap(jit(_searchsorted_scan_impl))/while/body/eval_jaxpr/gather | solution.py:85
  296.7 25.9 %gather_fusion.2 = s32[4096]{0:T(1024)S(1)} fusion(s32[512]{0:T(512)S(1)} %copy-done.1, s32[4096]{0:T(1024)S(1)} %fusion.38), kind=kCustom, calls=%fused_computation.2 | custom fusion | bytes 49152 | tf_op jit(solution)/shard_map/gather | solution.py:86
  328.4 22.5 %all_gather.22 = bf16[512,512]{1,0:T(8,128)(2,1)S(1)} all-gather(bf16[16,512]{1,0:T(8,128)(2,1)S(1)} %bitcast.112), channel_id=1, replica_groups=mesh['req'=32,'tp'=4] {'req'}, dimensions={0}, use_global_device_ids=true | all-gather | bytes 540672 | tf_op jit(solution)/shard_map/all_gather | solution.py:107
  351.0 17.3 %gather_fusion.3 = bf16[4096,512]{1,0:T(8,128)(2,1)} fusion(bf16[512,512]{1,0:T(8,128)(2,1)S(1)} %all_gather.22, s32[4096]{0:T(1024)S(1)} %broadcast_clamp_fusion.1), kind=kCustom, calls=%fused_computation.3 | custom fusion | bytes 8404992 | tf_op jit(solution)/shard_map/gather | solution.py:108
  425.5 14.4 %multiply_select_fusion = f32[4096,2,2]{2,1,0:T(2,128)S(1)} fusion(f32[4096,2,2]{2,1,0:T(2,128)S(1)} %bitcast.97, pred[4096]{0:T(1024)(128)(4,1)S(1)} %broadcast_compare_fusion), kind=kLoop, calls=%fused_computation.39 | loop fusion | flops 32768 | bytes 135168 | tf_op jit(solution)/shard_map/jit(_where)/select_n | solution.py:113
  463.9 28.3 %gather_fusion.4 = f32[4096,2,2]{2,1,0:T(2,128)} fusion(f32[512,2,2]{2,1,0:T(2,128)S(1)} %copy.93, s32[4096]{0:T(1024)S(1)} %broadcast_clamp_fusion.1), kind=kCustom, calls=%fused_computation.4 | custom fusion | bytes 147456 | tf_op jit(solution)/shard_map/gather | solution.py:119
  492.2 16.7 %exponential_select_fusion = f32[4096,2,2]{2,1,0:T(2,128)S(1)} fusion(f32[4096,2,2]{2,1,0:T(2,128)} %gather_fusion.4, pred[4096]{0:T(1024)(128)(4,1)S(1)} %broadcast_compare_fusion, f32[4096,2,2]{2,1,0:T(2,128)} %bitcast.98), kind=kLoop, calls=%fused_computation.38 | loop fusion | flops 65536 | bytes 200704 | tf_op jit(solution)/shard_map/jit(_where)/select_n | solution.py:119
  542.8 25.0 %all-gather = f32[16384,2,2]{0,2,1:T(2,128)S(1)} all-gather(f32[512,2,2]{0,2,1:T(2,128)S(1)} %pad_maximum_fusion.6), channel_id=2, replica_groups=mesh['req'=32,'tp'=4] {'req'}, dimensions={0}, use_global_device_ids=true | all-gather | bytes 270336 | tf_op jit(solution)/shard_map/all_gather | solution.py:14
  576.8 22.4 %all-gather.1 = f32[16384,2,2]{0,2,1:T(2,128)S(1)} all-gather(f32[512,2,2]{0,2,1:T(2,128)S(1)} %fusion.15), channel_id=3, replica_groups=mesh['req'=32,'tp'=4] {'req'}, dimensions={0}, use_global_device_ids=true | all-gather | bytes 270336 | tf_op jit(solution)/shard_map/all_gather | solution.py:14
  603.1 55.4 %all-gather.5.cloned.1.call-done = f32[16384,2,2,128]{3,0,2,1:T(8,128)} async-done(((f32[512,2,2,128]{3,0,2,1:T(8,128)}), f32[16384,2,2,128]{3,0,2,1:T(8,128)}) %all-gather.5.cloned.1.call-update) | async-done | bytes 33554448 | tf_op jit(solution)/shard_map/all_gather | solution.py:14
  661.5 362.1 %while.43 = (s32[]{:T(128)}, f32[512,2,2]{0,2,1:T(2,128)S(1)}, f32[512,2,2]{0,2,1:T(2,128)S(1)}, f32[512,2,2,128]{3,2,1,0:T(2,128)}, f32[32,512,2,2]{1,0,3,2:T(8...) while((s32[]{:T(128)}, f32[512,2,2]{0,2,1:T(2,128)S(1)}, ...), condition=%wide.region_8.9_spmd, body=%wide.region_7.8_spmd.sunk | while | flops 798725 | bytes 5390479 | solution.py:19
  1026.2 40.3 %all-reduce.4.cloned.1.call-done = f32[16,2048]{1,0:T(8,128)} async-done(((f32[16,2048]{1,0:T(8,128)}), f32[16,2048]{1,0:T(8,128)}) %all-reduce.4.cloned.1.call-update) | async-done | bytes 131088 | tf_op jit(solution)/shard_map/psum | solution.py:158
  1077.4 41.0 %all-reduce.6.cloned.1.call-done = f32[16,2048]{1,0:T(8,128)} async-done(((f32[16,2048]{1,0:T(8,128)}), f32[16,2048]{1,0:T(8,128)}) %all-reduce.6.cloned.1.call-update) | async-done | bytes 131088 | tf_op jit(solution)/shard_map/psum | solution.py:164
  (336 shorter events, 524.2 us)
Async XLA Ops:
  7.2 1017.8 %copy-start = (bf16[512,2048]{1,0:T(8,128)(2,1)S(1)}, bf16[512,2048]{1,0:T(8,128)(2,1)}, u32[]{:S(2)}) copy-start(bf16[512,2048]{1,0:T(8,128)(2,1)} %param.29) | copy-start | bytes 6291460
  7.2 651.3 %all-gather.5.cloned.1.call-start = ((), (), s32[]{:S(2)}) async-start(), calls=%async_computation.2 | async-start | bytes 34603008 | tf_op jit(solution)/shard_map/all_gather | solution.py:14
  296.0 0.7 copy-start.1
  322.6 5.1 copy-start.5
  322.6 5.0 copy-start.6
  425.5 14.5 %copy-start.3 = (f32[4096,2,1,2]{3,2,1,0:T(1,128)}, f32[4096,2,1,2]{3,2,1,0:T(1,128)S(1)}, u32[]{:S(2)}) copy-start(f32[4096,2,1,2]{3,2,1,0:T(1,128)S(1)} %fusion.57) | copy-start | bytes 196612
  508.9 5.1 copy-start.2
  518.5 11.7 %copy-start.4 = (bf16[4096,1,256]{0,2,1:T(8,128)(2,1)S(1)}, bf16[4096,1,256]{0,2,1:T(8,128)(2,1)}, u32[]{:S(2)}) copy-start(bf16[4096,1,256]{0,2,1:T(8,128)(2,1)} %copy.117) | copy-start | bytes 6291460
  542.8 523.6 %all-reduce.4.cloned.1.call-start = ((), (), s32[]{:S(2)}) async-start(), calls=%async_computation | async-start | bytes 262144 | tf_op jit(solution)/shard_map/psum | solution.py:158
  567.8 9.0 copy-start.8
  599.2 62.3 %slice-start = ((f32[16384,2,2]{0,2,1:T(2,128)}), f32[512,2,2]{0,2,1:T(2,128)S(1)}, s32[]{:S(2)}) async-start(f32[16384,2,2]{0,2,1:T(2,128)} %copy-done.8), calls=%async_computation.3 | async-start | bytes 16384 | tf_op jit(solution)/shard_map/jit(dynamic_index_in_dim)/dynamic_slice | solution.py:17
  661.5 364.6 %copy-start.9 = (bf16[2048]{0:T(1024)(128)(2,1)S(1)}, bf16[2048]{0:T(1024)(128)(2,1)}, u32[]{:S(2)}) copy-start(bf16[2048]{0:T(1024)(128)(2,1)} %param.30) | copy-start | bytes 12292
  1026.1 92.3 %all-reduce.6.cloned.1.call-start = ((), (), s32[]{:S(2)}) async-start(), calls=%async_computation.1 | async-start | bytes 262144 | tf_op jit(solution)/shard_map/psum | solution.py:164
  1071.3 47.1 %copy-start.7 = (f32[16,2048]{1,0:T(8,128)S(1)}, f32[16,2048]{1,0:T(8,128)}, u32[]{:S(2)}) copy-start(f32[16,2048]{1,0:T(8,128)} %all-reduce.4.cloned.1.call-done) | copy-start | bytes 393220
Sparse Core Ops, SparseCore 0:
  542.9 115.5 all-gather.4
  1026.2 40.1 all-reduce.3
  1076.8 41.5 all-reduce.5
where the time goes:
time: 1140 us; the launch traced here: 1130 us
  local copies, waits for them, and re-layouts  504 us (44%)
  other arithmetic  331 us (29%)
  waiting for transfers between devices  137 us (12%)
  blocking collectives  88.2 us (8%)
  matrix products  49.8 us (4%)
  between operations  15.1 us (1%)
    add x31, other arithmetic, combine_parts(): first[2] * left[..., None] + second[2] * right[..., None]  277 us
    gather x10, local copies, waits for them, and re-layouts, per_device(): place = jnp.searchsorted(ends, slot_ids, side='right')  259 us
    dynamic_slice x66, local copies, waits for them, and re-layouts, take(): lax.dynamic_index_in_dim(a, source, 0, False)  68.2 us
    all_gather x1, waiting for transfers between devices, joined(): gathered = jax.tree.map(lambda a: lax.all_gather(a, axis), part)  55.4 us
    all_gather x2, blocking collectives, joined(): gathered = jax.tree.map(lambda a: lax.all_gather(a, axis), part)  47.4 us
    psum x1, waiting for transfers between devices, per_device(): hidden_out = mid + lax.psum(down_part, 'tp')  41 us
    psum x1, waiting for transfers between devices, per_device(): mid = rows + lax.psum(partial_attn, 'tp')  40.3 us
    gather x1, local copies, waits for them, and re-layouts, per_device(): weights = jnp.where(live, jnp.exp(scores - peak[owner]), 0.0)  28.3 us
  transfers between devices with their start and end apart: 3, of which 3 were waited for; matrix products, arithmetic and copies ran while one was open for 1% of the time, Pallas kernels for 0%

commit v1 on v0

--- a/solution.py
+++ b/solution.py
@@ -161,7 +161,7 @@
     upper = jnp.dot(normed_mid, w_up, preferred_element_type=jnp.float32)
     act = (jax.nn.silu(gate) * upper).astype(jnp.bfloat16)
     down_part = jnp.dot(act, w_down, preferred_element_type=jnp.float32)
-    hidden_out = mid + lax.psum(down_part, "tp")
+    hidden_out = mid + jnp.sum(lax.all_gather(down_part, "tp"), axis=0)
     return (hidden_out, new_kv)
 
 

time: 1140 us -> 1110 us (0.974)
  waiting for transfers between devices: 137 us -> 95 us
  blocking collectives: 88.2 us -> 101 us
    psum x1 -> x0, waiting for transfers between devices: 41 us -> none  [per_device(): hidden_out = mid + lax.psum(down_part, 'tp')]
    all_gather x0 -> x1, blocking collectives: none -> 12.9 us  [per_device(): hidden_out = mid + jnp.sum(lax.all_gather(down_part, 'tp'), axis=0)]
  transfers between devices with their start and end apart: 3 -> 2, of which waited for: 3 -> 2; matrix products, arithmetic and copies ran while one was open for 1% -> 1% of each run, Pallas kernels for 0% -> 0%
where the time goes in v1:
time: 1110 us; the launch traced here: 1100 us
  local copies, waits for them, and re-layouts  505 us (45%)
  other arithmetic  331 us (30%)
  blocking collectives  101 us (9%)
  waiting for transfers between devices  95 us (9%)
  matrix products  49.1 us (4%)
  between operations  15.4 us (1%)
    add x31, other arithmetic, combine_parts(): first[2] * left[..., None] + second[2] * right[..., None]  278 us
    gather x10, local copies, waits for them, and re-layouts, per_device(): place = jnp.searchsorted(ends, slot_ids, side='right')  259 us
    dynamic_slice x66, local copies, waits for them, and re-layouts, take(): lax.dynamic_index_in_dim(a, source, 0, False)  68.2 us
    all_gather x1, waiting for transfers between devices, joined(): gathered = jax.tree.map(lambda a: lax.all_gather(a, axis), part)  55.4 us
    all_gather x2, blocking collectives, joined(): gathered = jax.tree.map(lambda a: lax.all_gather(a, axis), part)  47.4 us
    psum x1, waiting for transfers between devices, per_device(): mid = rows + lax.psum(partial_attn, 'tp')  39.6 us
    gather x1, local copies, waits for them, and re-layouts, per_device(): weights = jnp.where(live, jnp.exp(scores - peak[owner]), 0.0)  28.5 us
    gather x1, local copies, waits for them, and re-layouts, per_device(): owner = pool_order[place]  25.9 us
  transfers between devices with their start and end apart: 2, of which 2 were waited for; matrix products, arithmetic and copies ran while one was open for 1% of the time, Pallas kernels for 0%

profile of v1, /device:TPU:0, one launch (start us, length us, event | category | flops | bytes accessed | tf_op | source)
XLA Modules:
  0.0 1097.2 jit_solution(18326767959702533367)
XLA Ops:
  12.5 18.3 %all-reduce = s32[512]{0:T(512)S(1)} all-reduce(s32[512]{0:T(512)S(1)} %dynamic-update-slice), channel_id=1, replica_groups=mesh['req'=32,'tp'=4] {'req'}, use_global_device_ids=true, to_apply=%add | all-reduce | flops 512 | bytes 4096
  36.3 259.8 %while.44 = (s32[]{:T(128)}, u32[4096]{0:T(1024)S(1)}, u32[4096]{0:T(1024)S(1)}, s32[512]{0:T(512)S(1)}, s32[]{:T(128)}, /*index=5*/s32[]{:T(128)}, s32[]{:T(128)}, s32[]{}) while((s32[]{:T(128)}, u32[4096]{0:T(1024)S(1)}, u32[4096]{0:T(1024)S(1)}, s32[512]{0:T(512)S(1)}, s32[]{:T(128)}, /*index=5*/s32[]{:T(128)}, s32[]{:T(128)}, ...), condition=%wide.region_3.4_spmd.clone, body=%wide.region_2.3_spmd.clone.sunk | while | flops 81924 | bytes 254065 | solution.py:85
  36.3 25.9 %gather_fusion = s32[4096]{0:T(1024)S(1)} fusion(s32[512]{0:T(512)S(1)} %get-tuple-element.479, u32[4096]{0:T(1024)S(1)} %broadcast_clamp_fusion.3), kind=kCustom, calls=%fused_computation.clone.clone.1 | custom fusion | bytes 49152 | tf_op jit(solution)/shard_map/jit(searchsorted)/jit(_searchsorted_scan_impl)/vmap(jit(_searchsorted_scan_impl))/while/body/eval_jaxpr/gather | solution.py:85
  62.3 25.9 %gather_fusion = s32[4096]{0:T(1024)S(1)} fusion(s32[512]{0:T(512)S(1)} %get-tuple-element.479, u32[4096]{0:T(1024)S(1)} %broadcast_clamp_fusion.3), kind=kCustom, calls=%fused_computation.clone.clone.1 | custom fusion | bytes 49152 | tf_op jit(solution)/shard_map/jit(searchsorted)/jit(_searchsorted_scan_impl)/vmap(jit(_searchsorted_scan_impl))/while/body/eval_jaxpr/gather | solution.py:85
  88.2 25.9 %gather_fusion = s32[4096]{0:T(1024)S(1)} fusion(s32[512]{0:T(512)S(1)} %get-tuple-element.479, u32[4096]{0:T(1024)S(1)} %broadcast_clamp_fusion.3), kind=kCustom, calls=%fused_computation.clone.clone.1 | custom fusion | bytes 49152 | tf_op jit(solution)/shard_map/jit(searchsorted)/jit(_searchsorted_scan_impl)/vmap(jit(_searchsorted_scan_impl))/while/body/eval_jaxpr/gather | solution.py:85
  114.2 25.9 %gather_fusion = s32[4096]{0:T(1024)S(1)} fusion(s32[512]{0:T(512)S(1)} %get-tuple-element.479, u32[4096]{0:T(1024)S(1)} %broadcast_clamp_fusion.3), kind=kCustom, calls=%fused_computation.clone.clone.1 | custom fusion | bytes 49152 | tf_op jit(solution)/shard_map/jit(searchsorted)/jit(_searchsorted_scan_impl)/vmap(jit(_searchsorted_scan_impl))/while/body/eval_jaxpr/gather | solution.py:85
  140.2 25.9 %gather_fusion = s32[4096]{0:T(1024)S(1)} fusion(s32[512]{0:T(512)S(1)} %get-tuple-element.479, u32[4096]{0:T(1024)S(1)} %broadcast_clamp_fusion.3), kind=kCustom, calls=%fused_computation.clone.clone.1 | custom fusion | bytes 49152 | tf_op jit(solution)/shard_map/jit(searchsorted)/jit(_searchsorted_scan_impl)/vmap(jit(_searchsorted_scan_impl))/while/body/eval_jaxpr/gather | solution.py:85
  166.2 25.9 %gather_fusion = s32[4096]{0:T(1024)S(1)} fusion(s32[512]{0:T(512)S(1)} %get-tuple-element.479, u32[4096]{0:T(1024)S(1)} %broadcast_clamp_fusion.3), kind=kCustom, calls=%fused_computation.clone.clone.1 | custom fusion | bytes 49152 | tf_op jit(solution)/shard_map/jit(searchsorted)/jit(_searchsorted_scan_impl)/vmap(jit(_searchsorted_scan_impl))/while/body/eval_jaxpr/gather | solution.py:85
  192.2 25.9 %gather_fusion = s32[4096]{0:T(1024)S(1)} fusion(s32[512]{0:T(512)S(1)} %get-tuple-element.479, u32[4096]{0:T(1024)S(1)} %broadcast_clamp_fusion.3), kind=kCustom, calls=%fused_computation.clone.clone.1 | custom fusion | bytes 49152 | tf_op jit(solution)/shard_map/jit(searchsorted)/jit(_searchsorted_scan_impl)/vmap(jit(_searchsorted_scan_impl))/while/body/eval_jaxpr/gather | solution.py:85
  218.1 25.9 %gather_fusion = s32[4096]{0:T(1024)S(1)} fusion(s32[512]{0:T(512)S(1)} %get-tuple-element.479, u32[4096]{0:T(1024)S(1)} %broadcast_clamp_fusion.3), kind=kCustom, calls=%fused_computation.clone.clone.1 | custom fusion | bytes 49152 | tf_op jit(solution)/shard_map/jit(searchsorted)/jit(_searchsorted_scan_impl)/vmap(jit(_searchsorted_scan_impl))/while/body/eval_jaxpr/gather | solution.py:85
  244.1 25.9 %gather_fusion = s32[4096]{0:T(1024)S(1)} fusion(s32[512]{0:T(512)S(1)} %get-tuple-element.479, u32[4096]{0:T(1024)S(1)} %broadcast_clamp_fusion.3), kind=kCustom, calls=%fused_computation.clone.clone.1 | custom fusion | bytes 49152 | tf_op jit(solution)/shard_map/jit(searchsorted)/jit(_searchsorted_scan_impl)/vmap(jit(_searchsorted_scan_impl))/while/body/eval_jaxpr/gather | solution.py:85
  270.1 25.9 %gather_fusion = s32[4096]{0:T(1024)S(1)} fusion(s32[512]{0:T(512)S(1)} %get-tuple-element.479, u32[4096]{0:T(1024)S(1)} %broadcast_clamp_fusion.3), kind=kCustom, calls=%fused_computation.clone.clone.1 | custom fusion | bytes 49152 | tf_op jit(solution)/shard_map/jit(searchsorted)/jit(_searchsorted_scan_impl)/vmap(jit(_searchsorted_scan_impl))/while/body/eval_jaxpr/gather | solution.py:85
  296.7 25.9 %gather_fusion.2 = s32[4096]{0:T(1024)S(1)} fusion(s32[512]{0:T(512)S(1)} %copy-done.1, s32[4096]{0:T(1024)S(1)} %fusion.38), kind=kCustom, calls=%fused_computation.2 | custom fusion | bytes 49152 | tf_op jit(solution)/shard_map/gather | solution.py:86
  328.4 22.5 %all_gather.28 = bf16[512,512]{1,0:T(8,128)(2,1)S(1)} all-gather(bf16[16,512]{1,0:T(8,128)(2,1)S(1)} %bitcast.114), channel_id=1, replica_groups=mesh['req'=32,'tp'=4] {'req'}, dimensions={0}, use_global_device_ids=true | all-gather | bytes 540672 | tf_op jit(solution)/shard_map/all_gather | solution.py:107
  350.9 17.3 %gather_fusion.3 = bf16[4096,512]{1,0:T(8,128)(2,1)} fusion(bf16[512,512]{1,0:T(8,128)(2,1)S(1)} %all_gather.28, s32[4096]{0:T(1024)S(1)} %broadcast_clamp_fusion.1), kind=kCustom, calls=%fused_computation.3 | custom fusion | bytes 8404992 | tf_op jit(solution)/shard_map/gather | solution.py:108
  425.4 14.4 %multiply_select_fusion = f32[4096,2,2]{2,1,0:T(2,128)S(1)} fusion(f32[4096,2,2]{2,1,0:T(2,128)S(1)} %bitcast.98, pred[4096]{0:T(1024)(128)(4,1)S(1)} %broadcast_compare_fusion), kind=kLoop, calls=%fused_computation.39 | loop fusion | flops 32768 | bytes 135168 | tf_op jit(solution)/shard_map/jit(_where)/select_n | solution.py:113
  463.8 28.5 %gather_fusion.4 = f32[4096,2,2]{2,1,0:T(2,128)} fusion(f32[512,2,2]{2,1,0:T(2,128)S(1)} %copy.93, s32[4096]{0:T(1024)S(1)} %broadcast_clamp_fusion.1), kind=kCustom, calls=%fused_computation.4 | custom fusion | bytes 147456 | tf_op jit(solution)/shard_map/gather | solution.py:119
  492.3 16.7 %exponential_select_fusion = f32[4096,2,2]{2,1,0:T(2,128)S(1)} fusion(f32[4096,2,2]{2,1,0:T(2,128)} %gather_fusion.4, pred[4096]{0:T(1024)(128)(4,1)S(1)} %broadcast_compare_fusion, f32[4096,2,2]{2,1,0:T(2,128)} %bitcast.99), kind=kLoop, calls=%fused_computation.38 | loop fusion | flops 65536 | bytes 200704 | tf_op jit(solution)/shard_map/jit(_where)/select_n | solution.py:119
  542.9 25.0 %all-gather = f32[16384,2,2]{0,2,1:T(2,128)S(1)} all-gather(f32[512,2,2]{0,2,1:T(2,128)S(1)} %pad_maximum_fusion.6), channel_id=2, replica_groups=mesh['req'=32,'tp'=4] {'req'}, dimensions={0}, use_global_device_ids=true | all-gather | bytes 270336 | tf_op jit(solution)/shard_map/all_gather | solution.py:14
  576.8 22.4 %all-gather.1 = f32[16384,2,2]{0,2,1:T(2,128)S(1)} all-gather(f32[512,2,2]{0,2,1:T(2,128)S(1)} %fusion.15), channel_id=3, replica_groups=mesh['req'=32,'tp'=4] {'req'}, dimensions={0}, use_global_device_ids=true | all-gather | bytes 270336 | tf_op jit(solution)/shard_map/all_gather | solution.py:14
  603.1 55.4 %all-gather.6.cloned.1.call-done = f32[16384,2,2,128]{3,0,2,1:T(8,128)} async-done(((f32[512,2,2,128]{3,0,2,1:T(8,128)}), f32[16384,2,2,128]{3,0,2,1:T(8,128)}) %all-gather.6.cloned.1.call-update) | async-done | bytes 33554448 | tf_op jit(solution)/shard_map/all_gather | solution.py:14
  661.6 362.5 %while.43 = (s32[]{:T(128)}, f32[512,2,2]{0,2,1:T(2,128)S(1)}, f32[512,2,2]{0,2,1:T(2,128)S(1)}, f32[512,2,2,128]{3,2,1,0:T(2,128)}, f32[32,512,2,2]{1,0,3,2:T(8...) while((s32[]{:T(128)}, f32[512,2,2]{0,2,1:T(2,128)S(1)}, ...), condition=%wide.region_8.9_spmd, body=%wide.region_7.8_spmd.sunk | while | flops 798725 | bytes 5390479 | solution.py:19
  1027.2 39.6 %all-reduce.3.cloned.1.call-done = f32[16,2048]{1,0:T(8,128)} async-done(((f32[16,2048]{1,0:T(8,128)}), f32[16,2048]{1,0:T(8,128)}) %all-reduce.3.cloned.1.call-update) | async-done | bytes 131088 | tf_op jit(solution)/shard_map/psum | solution.py:158
  1076.4 12.9 %all-gather.3 = f32[64,2048]{1,0:T(8,128)S(1)} all-gather(f32[16,2048]{1,0:T(8,128)S(1)} %fusion.26), channel_id=5, replica_groups=mesh['req'=32,'tp'=4] {'tp'}, dimensions={0}, use_global_device_ids=true | all-gather | bytes 655360 | tf_op jit(solution)/shard_map/all_gather | solution.py:164
  (335 shorter events, 522.8 us)
Async XLA Ops:
  7.2 1018.2 %copy-start = (bf16[512,2048]{1,0:T(8,128)(2,1)S(1)}, bf16[512,2048]{1,0:T(8,128)(2,1)}, u32[]{:S(2)}) copy-start(bf16[512,2048]{1,0:T(8,128)(2,1)} %param.29) | copy-start | bytes 6291460
  7.2 651.3 %all-gather.6.cloned.1.call-start = ((), (), s32[]{:S(2)}) async-start(), calls=%async_computation.1 | async-start | bytes 34603008 | tf_op jit(solution)/shard_map/all_gather | solution.py:14
  296.0 0.7 copy-start.1
  322.6 5.0 copy-start.5
  322.6 5.0 copy-start.6
  425.4 14.5 %copy-start.3 = (f32[4096,2,1,2]{3,2,1,0:T(1,128)}, f32[4096,2,1,2]{3,2,1,0:T(1,128)S(1)}, u32[]{:S(2)}) copy-start(f32[4096,2,1,2]{3,2,1,0:T(1,128)S(1)} %fusion.57) | copy-start | bytes 196612
  509.0 5.1 copy-start.2
  518.5 11.7 %copy-start.4 = (bf16[4096,1,256]{0,2,1:T(8,128)(2,1)S(1)}, bf16[4096,1,256]{0,2,1:T(8,128)(2,1)}, u32[]{:S(2)}) copy-start(bf16[4096,1,256]{0,2,1:T(8,128)(2,1)} %copy.117) | copy-start | bytes 6291460
  542.8 524.0 %all-reduce.3.cloned.1.call-start = ((), (), s32[]{:S(2)}) async-start(), calls=%async_computation | async-start | bytes 262144 | tf_op jit(solution)/shard_map/psum | solution.py:158
  567.9 9.0 copy-start.8
  599.3 62.3 %slice-start = ((f32[16384,2,2]{0,2,1:T(2,128)}), f32[512,2,2]{0,2,1:T(2,128)S(1)}, s32[]{:S(2)}) async-start(f32[16384,2,2]{0,2,1:T(2,128)} %copy-done.8), calls=%async_computation.2 | async-start | bytes 16384 | tf_op jit(solution)/shard_map/jit(dynamic_index_in_dim)/dynamic_slice | solution.py:17
  661.6 364.9 %copy-start.9 = (bf16[2048]{0:T(1024)(128)(2,1)S(1)}, bf16[2048]{0:T(1024)(128)(2,1)}, u32[]{:S(2)}) copy-start(bf16[2048]{0:T(1024)(128)(2,1)} %param.30) | copy-start | bytes 12292
  1071.7 17.7 %copy-start.7 = (f32[16,2048]{1,0:T(8,128)S(1)}, f32[16,2048]{1,0:T(8,128)}, u32[]{:S(2)}) copy-start(f32[16,2048]{1,0:T(8,128)} %all-reduce.3.cloned.1.call-done) | copy-start | bytes 393220
Sparse Core Ops, SparseCore 0:
  542.9 115.5 all-gather.5
  1026.6 40.1 all-reduce.2
